TPU v7x, 32 devices: a whole 2x2x4 slice. The times are simulated.
32 devices in a mesh: row: 4 (over z), col: 8 (over y, x, core).
Axes of the slice: x: 2, y: 2, z: 4, core: 2. Of those that a mesh axis runs over, the one named last changes fastest.
Arguments:
- b_tensor: bfloat16 [128, 512, 512], P('col', 'row'), may hold values from -0.4 to 0.4, as said below
- ri_pairs: int32 [128, 4, 4], P('col'), may hold values from 0 to 1, as said below
- g_occ: bfloat16 [512, 512], P(None, 'col'), may hold values from -0.25 to 0.25
- g_vir: bfloat16 [512, 512], P(None, 'col'), may hold values from -0.25 to 0.25
- occ_mask: int32 [4, 4], replicated, may hold values 0 or 1
- vir_mask: int32 [4, 4], replicated, may hold values 0 or 1
Outputs:
- chi: float32 [128, 128], P('col', 'row')
Inputs may be any that keep to these rules, and one draw needn't show every extreme that they name: b_tensor[p] is a symmetric matrix for every p. ri_pairs[p] is symmetric with ones on its diagonal.
All inputs are finite; a program needn't handle non-finite values.
Results may differ from a plain program's by a relative error of at most 0.004.
Values may be sent and summed in bfloat16 or wider, within the bound.
A program may use at most 64 MiB of HBM per device.

v0:
```python
import jax
import jax.numpy as jnp
from jax import lax
from jax.sharding import PartitionSpec as P

BS = 128
NA_ROW = 1


def spread(mask, block):
    shape = mask.shape
    widened = jnp.broadcast_to(
        mask[..., :, None, :, None], shape[:-2] + (shape[-2], block, shape[-1], block)
    )
    return widened.reshape(shape[:-2] + (shape[-2] * block, shape[-1] * block))


def body(b_tensor, ri_pairs, g_occ, g_vir, occ_mask, vir_mask):
    row_index = lax.axis_index("row")
    pattern = lax.dynamic_slice_in_dim(ri_pairs, row_index * NA_ROW, NA_ROW, 1)
    masked = b_tensor * spread(pattern, BS).astype(jnp.bfloat16)
    occ_full, vir_full = (
        lax.all_gather(g_occ, "col", axis=1, tiled=True),
        lax.all_gather(g_vir, "col", axis=1, tiled=True),
    )
    occ_green = occ_full * spread(occ_mask, BS).astype(jnp.bfloat16)
    vir_green = vir_full * spread(vir_mask, BS).astype(jnp.bfloat16)
    occ_side = jnp.einsum(
        "lm,pnm->pln", occ_green, masked, preferred_element_type=jnp.float32
    ).astype(jnp.bfloat16)
    vir_side = jnp.einsum(
        "pls,sn->pln", masked, vir_green, preferred_element_type=jnp.float32
    ).astype(jnp.bfloat16)
    vir_moved = lax.all_to_all(vir_side, "row", split_axis=2, concat_axis=1, tiled=True)
    occ_parts, vir_parts = (
        lax.all_to_all(occ_side, "col", split_axis=1, concat_axis=0, tiled=True),
        lax.all_to_all(vir_moved, "col", split_axis=1, concat_axis=0, tiled=True),
    )
    total_ri = occ_parts.shape[0]
    occ_flat = occ_parts.reshape(total_ri, -1)
    vir_flat = vir_parts.reshape(total_ri, -1)
    chi_part = lax.psum_scatter(
        lax.dot_general(
            occ_flat, vir_flat, (((1,), (1,)), ((), ())), preferred_element_type=jnp.float32
        ),
        "col",
        scatter_dimension=0,
        tiled=True,
    )
    return lax.psum_scatter(chi_part, "row", scatter_dimension=1, tiled=True)


def solution(mesh):
    in_specs = (
        P("col", "row", None),
        P("col", None, None),
        P(None, "col"),
        P(None, "col"),
        P(),
        P(),
    )
    out_specs = P("col", "row")
    return jax.shard_map(body, mesh=mesh, in_specs=in_specs, out_specs=out_specs, check_vma=False)
```

profile of v0, /device:TPU:0, one launch (start us, length us, event | category | flops | bytes accessed | tf_op | source)
XLA Modules:
  0.0 205.6 jit_solution(296959257917255774)
XLA Ops:
  6.5 0.7 convert_element_type.41
  7.2 0.1 copy.38
  7.3 0.7 fusion.15
  8.0 0.1 copy.32
  8.1 0.1 broadcast_in_dim.8
  8.2 11.6 %all_gather.7 = bf16[512,512]{0,1:T(8,128)(2,1)S(1)} all-gather(bf16[512,64]{0,1:T(8,128)(2,1)} %param.9), channel_id=1, replica_groups=mesh['row'=4,'col'=8] {'col'}, dimensions={1}, use_global_device_ids=true | all-gather | bytes 589824 | tf_op jit(solution)/shard_map/all_gather | solution.py:24
  19.8 0.2 broadcast_in_dim.11
  20.0 2.9 %convolution_convert_fusion = bf16[16,128,512]{2,1,0:T(8,128)(2,1)S(1)} fusion(bf16[16,128,512]{2,1,0:T(8,128)(2,1)} %param.6, bf16[16,512]{1,0:T(8,128)(2,1)S(1)} %bitcast.64, bf16[512,512]{0,1:T(8,128)(2,1)S(1)} %all_gather.7, bf16[64,8,4,128]{3,2,1,0:T(4,128)(2,1)S(1)} %bitcast.60), kind=kOutput, calls=%fused_computation.6 | convolution fusion | flops 1076101120 | bytes 5259264 | tf_op jit(solution)/shard_map/pls,sn->pln/dot_general | solution.py:31
  22.9 3.1 %copy.40 = bf16[16,128,512]{1,0,2:T(8,128)(2,1)} copy(bf16[16,128,512]{2,1,0:T(8,128)(2,1)S(1)} %convolution_convert_fusion) | data formatting | bytes 4194304 | tf_op jit(solution)/shard_map/convert_element_type | solution.py:33
  26.0 5.0 %all-to-all-start.1 = ((bf16[16,128,512]{1,0,2:T(8,128)(2,1)}), bf16[16,128,512]{1,0,2:T(8,128)(2,1)S(1)}, u32[]{:S(2)}, u32[]{:S(2)}) async-start(bf16[16,128,512]{1,0,2:T(8,128)(2,1)} %copy.40), calls=%async_computation.1 | async-start | bytes 4194304 | tf_op jit(solution)/shard_map/all_to_all | solution.py:34
  31.0 0.1 copy.33
  31.1 9.5 %all_gather.6 = bf16[512,512]{0,1:T(8,128)(2,1)S(1)} all-gather(bf16[512,64]{0,1:T(8,128)(2,1)S(1)} %copy-done.1), channel_id=1, replica_groups=mesh['row'=4,'col'=8] {'col'}, dimensions={1}, use_global_device_ids=true | all-gather | bytes 589824 | tf_op jit(solution)/shard_map/all_gather | solution.py:23
  40.7 0.2 broadcast_in_dim.10
  40.9 4.2 %convert_bitcast_fusion = bf16[16,512,128]{1,2,0:T(8,128)(2,1)} fusion(bf16[16,128,512]{2,1,0:T(8,128)(2,1)} %param.6, bf16[16,512]{1,0:T(8,128)(2,1)S(1)} %bitcast.65, bf16[512,512]{0,1:T(8,128)(2,1)S(1)} %all_gather.6, bf16[64,8,4,128]{3,2,1,0:T(4,128)(2,1)S(1)} %bitcast.59), kind=kOutput, calls=%fused_computation.5 | convolution fusion | flops 1076101120 | bytes 5259264 | tf_op jit(solution)/shard_map/lm,pnm->pln/dot_general | solution.py:28
  45.1 4.5 %copy.35 = bf16[16,512,128]{2,0,1:T(8,128)(2,1)} copy(bf16[16,512,128]{1,2,0:T(8,128)(2,1)} %convert_bitcast_fusion) | data formatting | bytes 4194304 | tf_op jit(solution)/shard_map/convert_element_type | solution.py:30
  49.5 30.2 %all-to-all-done.1 = bf16[16,128,512]{1,0,2:T(8,128)(2,1)S(1)} async-done(((bf16[16,128,512]{1,0,2:T(8,128)(2,1)}), bf16[16,128,512]{1,0,2:T(8,128)(2,1)S(1)}, u32[]{:S(2)}, u32[]{:S(2)}) %all-to-all-start.1) | async-done | bytes 2097184 | tf_op jit(solution)/shard_map/all_to_all | solution.py:34
  79.7 4.3 %all-to-all-start = ((bf16[16,512,128]{2,0,1:T(8,128)(2,1)}), bf16[16,512,128]{2,0,1:T(8,128)(2,1)}, u32[]{:S(2)}, u32[]{:S(2)}) async-start(bf16[16,512,128]{2,0,1:T(8,128)(2,1)} %copy.35), calls=%async_computation | async-start | bytes 4194304 | tf_op jit(solution)/shard_map/all_to_all | solution.py:36
  84.1 3.7 %copy.51 = bf16[16,4,128,128]{3,0,2,1:T(8,128)(2,1)} copy(bf16[16,4,128,128]{2,0,3,1:T(8,128)(2,1)S(1)} %bitcast.54) | data formatting | bytes 4194304 | tf_op jit(solution)/shard_map/all_to_all | solution.py:34
  87.8 22.9 %all-to-all-done = bf16[16,512,128]{2,0,1:T(8,128)(2,1)} async-done(((bf16[16,512,128]{2,0,1:T(8,128)(2,1)}), bf16[16,512,128]{2,0,1:T(8,128)(2,1)}, u32[]{:S(2)}, u32[]{:S(2)}) %all-to-all-start) | async-done | bytes 2097184 | tf_op jit(solution)/shard_map/all_to_all | solution.py:36
  110.7 3.6 %all-to-all-start.2 = ((bf16[16,512,128]{2,0,1:T(8,128)(2,1)}), bf16[16,512,128]{2,0,1:T(8,128)(2,1)S(1)}, u32[]{:S(2)}, u32[]{:S(2)}) async-start(bf16[16,512,128]{2,0,1:T(8,128)(2,1)} %bitcast.55), calls=%async_computation.2 | async-start | bytes 4194304 | tf_op jit(solution)/shard_map/all_to_all | solution.py:37
  114.3 0.0 reduce-scatter.5.cloned.1.call-start
  114.4 3.5 %copy.37 = bf16[8,16,64,128]{3,2,1,0:T(8,128)(2,1)} copy(bf16[8,16,64,128]{3,1,2,0:T(8,128)(2,1)} %bitcast.5) | data formatting | bytes 4194304 | tf_op jit(solution)/shard_map/all_to_all | solution.py:36
  117.9 23.1 %all-to-all-done.2 = bf16[16,512,128]{2,0,1:T(8,128)(2,1)S(1)} async-done(((bf16[16,512,128]{2,0,1:T(8,128)(2,1)}), bf16[16,512,128]{2,0,1:T(8,128)(2,1)S(1)}, u32[]{:S(2)}, u32[]{:S(2)}) %all-to-all-start.2) | async-done | bytes 2097184 | tf_op jit(solution)/shard_map/all_to_all | solution.py:37
  140.9 0.5 copy.44
  141.5 1.0 copy-done
  142.5 2.9 %fusion = f32[128,128]{1,0:T(8,128)} fusion(bf16[16,8,64,128]{3,2,1,0:T(8,128)(2,1)S(1)} %bitcast.58, bf16[16,8,64,128]{3,2,1,0:T(8,128)(2,1)S(1)} %bitcast.57), kind=kOutput, calls=%fused_computation | convolution fusion | flops 268435456 | bytes 4259840 | tf_op jit(solution)/shard_map/dot_general | solution.py:43
  145.4 0.0 reduce-scatter.5.cloned.1.call-update
  145.4 0.0 reduce-scatter.7.cloned.1.call-start
  145.5 30.6 %reduce-scatter.5.cloned.1.call-done = f32[16,128]{1,0:T(8,128)} async-done(((f32[128,128]{1,0:T(8,128)}), f32[16,128]{1,0:T(8,128)}) %reduce-scatter.5.cloned.1.call-update) | async-done | bytes 8208 | tf_op jit(solution)/shard_map/reduce_scatter | solution.py:42
  176.0 1.4 copy.52
  177.5 19.9 %reduce-scatter.7.cloned.1.call-done = f32[32,16]{1,0:T(8,128)} async-done(((f32[128,16]{1,0:T(8,128)}), f32[32,16]{1,0:T(8,128)}) %reduce-scatter.7.cloned.1.call-update) | async-done | bytes 2064
  197.4 1.4 copy.53
  (8 shorter events, 0.0 us)
Async XLA Ops:
  26.0 5.0 %copy-start.2 = (s32[4,4]{1,0:T(4,128)S(1)}, s32[4,4]{1,0:T(4,128)}, u32[]{:S(2)}) copy-start(s32[4,4]{1,0:T(4,128)} %param.10) | copy-start | bytes 196
  26.0 5.1 %copy-start.1 = (bf16[512,64]{0,1:T(8,128)(2,1)S(1)}, bf16[512,64]{0,1:T(8,128)(2,1)}, u32[]{:S(2)}) copy-start(bf16[512,64]{0,1:T(8,128)(2,1)} %param.8) | copy-start | bytes 196612
  26.0 53.7 %all-to-all-start.1 = ((bf16[16,128,512]{1,0,2:T(8,128)(2,1)}), bf16[16,128,512]{1,0,2:T(8,128)(2,1)S(1)}, u32[]{:S(2)}, u32[]{:S(2)}) async-start(bf16[16,128,512]{1,0,2:T(8,128)(2,1)} %copy.40), calls=%async_computation.1 | async-start | bytes 4194304 | tf_op jit(solution)/shard_map/all_to_all | solution.py:34
  79.7 31.0 %all-to-all-start = ((bf16[16,512,128]{2,0,1:T(8,128)(2,1)}), bf16[16,512,128]{2,0,1:T(8,128)(2,1)}, u32[]{:S(2)}, u32[]{:S(2)}) async-start(bf16[16,512,128]{2,0,1:T(8,128)(2,1)} %copy.35), calls=%async_computation | async-start | bytes 4194304 | tf_op jit(solution)/shard_map/all_to_all | solution.py:36
  110.7 30.2 %all-to-all-start.2 = ((bf16[16,512,128]{2,0,1:T(8,128)(2,1)}), bf16[16,512,128]{2,0,1:T(8,128)(2,1)S(1)}, u32[]{:S(2)}, u32[]{:S(2)}) async-start(bf16[16,512,128]{2,0,1:T(8,128)(2,1)} %bitcast.55), calls=%async_computation.2 | async-start | bytes 4194304 | tf_op jit(solution)/shard_map/all_to_all | solution.py:37
  114.3 61.7 %reduce-scatter.5.cloned.1.call-start = ((), (), s32[]{:S(2)}) async-start(), calls=%async_computation.5 | async-start | bytes 73728 | tf_op jit(solution)/shard_map/reduce_scatter | solution.py:42
  140.9 1.6 copy-start
  145.4 52.0 %reduce-scatter.7.cloned.1.call-start = ((), (), s32[]{:S(2)}) async-start(), calls=%async_computation.6 | async-start | bytes 81920
Sparse Core Ops, SparseCore 0:
  145.5 30.4 reduce-scatter.4
  178.3 18.9 reduce-scatter.6
where the time goes:
time: 206 us
  waiting for transfers between devices  127 us (62%)
  blocking collectives  21.1 us (10%)
  local copies, waits for them, and re-layouts  20 us (10%)
  between operations  13.5 us (7%)
  starting transfers between devices  13 us (6%)
  matrix products  9.97 us (5%)
    reduce_scatter x1, waiting for transfers between devices, body(): lax.psum_scatter(lax.dot_general(occ_flat, vir_flat, (((1,), (1,)), ((),...  30.6 us
    all_to_all x1, waiting for transfers between devices, body(): lax.all_to_all(vir_side, 'row', split_axis=2, concat_axis=1, tiled=True)  30.2 us
    all_to_all x1, waiting for transfers between devices, body(): lax.all_to_all(vir_moved, 'col', split_axis=1, concat_axis=0, tiled=True)  23.1 us
    all_to_all x1, waiting for transfers between devices, body(): lax.all_to_all(occ_side, 'col', split_axis=1, concat_axis=0, tiled=True)  22.9 us
    unnamed x3, waiting for transfers between devices  19.9 us
    all_gather x1, blocking collectives, body(): lax.all_gather(g_vir, 'col', axis=1, tiled=True)  11.6 us
    all_gather x1, blocking collectives, body(): lax.all_gather(g_occ, 'col', axis=1, tiled=True)  9.54 us
    all_to_all x1, starting transfers between devices, body(): lax.all_to_all(vir_side, 'row', split_axis=2, concat_axis=1, tiled=True)  5 us
  transfers between devices with their start and end apart: 5, of which 5 were waited for; matrix products, arithmetic and copies ran while one was open for 8% of the time, Pallas kernels for 0%

commit v1 on v0

v1 whole, which is shorter than its diff:
```python
import functools

import jax
import jax.numpy as jnp
from jax import lax
from jax.experimental import pallas as pl
from jax.experimental.pallas import tpu as pltpu
from jax.sharding import PartitionSpec as P

BS = 128


def kernel(nr, nc, ri_ref, om_ref, vm_ref, b_ref, go_ref, gv_ref, out_ref,
           gv_slots, go_slots, gv, go, wide, v16, o16, vir_all, occ_all,
           chi, red1, st2, red2,
           g_send, g_recv, v_send, v_recv, o_send, o_recv,
           r1_send, r1_recv, r2_send, r2_recv):
    r = lax.axis_index("row")
    c = lax.axis_index("col")
    me = r * nc + c
    n_dev = nr * nc
    np_, rows, n = b_ref.shape
    na = n // BS
    pc = rows // nc
    packed = gv_ref.shape[0]
    q = n // packed
    w = n // nc

    def remote(src, dst, send, recv, row, col):
        return pltpu.make_async_remote_copy(
            src_ref=src, dst_ref=dst, send_sem=send, recv_sem=recv,
            device_id={"row": row, "col": col}, device_id_type=pl.DeviceIdType.MESH)

    barrier = pltpu.get_barrier_semaphore()

    def greet(i, _):
        t = lax.rem(me + i, n_dev)
        pl.semaphore_signal(barrier, inc=1,
                            device_id={"row": t // nc, "col": lax.rem(t, nc)},
                            device_id_type=pl.DeviceIdType.MESH)
        return 0

    lax.fori_loop(1, n_dev, greet, 0)
    pl.semaphore_wait(barrier, n_dev - 1)

    def g_copy(i, kind):
        t = lax.rem(c + i, nc)
        src, dst = (gv_ref, gv_slots) if kind == 0 else (go_ref, go_slots)
        return remote(src, dst.at[c], g_send.at[kind, i], g_recv.at[kind, i], r, t)

    for kind in (0, 1):
        def g_start(i, _):
            g_copy(i, kind).start()
            return 0
        lax.fori_loop(1, nc, g_start, 0)
    gv_slots[pl.ds(c, 1)] = gv_ref[...][None]
    go_slots[pl.ds(c, 1)] = go_ref[...][None]

    def assemble(kind, slots, full, mask):
        def g_wait(i, _):
            g_copy(i, kind).wait_recv()
            return 0
        lax.fori_loop(1, nc, g_wait, 0)
        per = BS // w
        for i in range(q):
            for j in range(na):
                block = jnp.concatenate(
                    [slots[j * per + k][:, i * w:(i + 1) * w] for k in range(per)], axis=1)
                for h in range(packed // BS):
                    m = mask[(i * packed // BS + h) * na + j].astype(jnp.float32)
                    piece = block[h * BS:(h + 1) * BS].astype(jnp.float32) * m
                    full[i * packed + h * BS:i * packed + (h + 1) * BS,
                         j * BS:(j + 1) * BS] = piece.astype(jnp.bfloat16)

    assemble(0, gv_slots, gv, vm_ref)

    def round_rows(dst):
        def one(i, _):
            for s in range(nr):
                dst[s, pl.ds(i * pc, pc)] = wide[s, pl.ds(i * pc, pc)].astype(jnp.bfloat16)
            return 0
        lax.fori_loop(0, nc, one, 0)

    for p in range(np_):
        row = jnp.concatenate(
            [jnp.full((1, BS), ri_ref[(p * na + r) * na + j].astype(jnp.float32)) for j in range(na)],
            axis=1)
        bm = (b_ref[p].astype(jnp.float32) * row).astype(jnp.bfloat16)

        res = jnp.dot(bm, gv[...], preferred_element_type=jnp.float32)
        for s in range(nr):
            wide[s, :, p, :] = res[:, s * BS:(s + 1) * BS]
    round_rows(v16)

    def v_copy(i):
        t = lax.rem(me + i, n_dev)
        tr, tc = t // nc, lax.rem(t, nc)
        return remote(v16.at[tr, pl.ds(tc * pc, pc)], vir_all.at[r, :, c],
                      v_send.at[i], v_recv.at[r, c], tr, tc)

    def v_start(i, _):
        v_copy(i).start()
        return 0

    lax.fori_loop(1, n_dev, v_start, 0)
    vir_all[pl.ds(r, 1), :, pl.ds(c, 1)] = v16[pl.ds(r, 1), pl.ds(c * pc, pc)][:, :, None]

    assemble(1, go_slots, go, om_ref)
    for p in range(np_):
        row = jnp.concatenate(
            [jnp.full((1, BS), ri_ref[(p * na + r) * na + j].astype(jnp.float32)) for j in range(na)],
            axis=1)
        bm = (b_ref[p].astype(jnp.float32) * row).astype(jnp.bfloat16)
        res = lax.dot_general(go[...], bm, (((1,), (1,)), ((), ())),
                              preferred_element_type=jnp.float32)
        for s in range(nr):
            wide[s, :, p, :] = res[s * BS:(s + 1) * BS]
    round_rows(o16)

    def o_copy(i):
        t = lax.rem(c + i, nc)
        return remote(o16.at[:, pl.ds(t * pc, pc)], occ_all.at[:, :, c],
                      o_send.at[i], o_recv.at[i], r, t)

    def o_start(i, _):
        o_copy(i).start()
        return 0

    lax.fori_loop(1, nc, o_start, 0)
    occ_all[:, :, pl.ds(c, 1)] = o16[:, pl.ds(c * pc, pc)][:, :, None]

    def o_wait(i, _):
        o_copy(i).wait_recv()
        return 0

    lax.fori_loop(1, nc, o_wait, 0)

    total_ri = nc * np_
    chi[...] = jnp.zeros_like(chi)
    step = min(pc, 8)
    for off in range(nr):
        rr = lax.rem(r + off, nr)

        def v_wait(j, _):
            col = lax.rem(c + j, nc)
            remote(v16.at[0, pl.ds(0, pc)], vir_all.at[rr, :, col],
                   v_send.at[0], v_recv.at[rr, col], rr, col).wait_recv()
            return 0

        lax.fori_loop(1 if off == 0 else 0, nc, v_wait, 0)
        for k in range(0, pc, step):
            left = occ_all[rr, k:k + step].reshape(step, total_ri, BS)
            right = vir_all[rr, k:k + step].reshape(step, total_ri, BS)
            left = jnp.concatenate([left[i] for i in range(step)], axis=1)
            right = jnp.concatenate([right[i] for i in range(step)], axis=1)
            chi[...] += lax.dot_general(
                left, right, (((1,), (1,)), ((), ())),
                preferred_element_type=jnp.float32).reshape(nc, np_, total_ri)

    def r1_copy(i):
        t = lax.rem(c + i, nc)
        return remote(chi.at[t], red1.at[c], r1_send.at[i], r1_recv.at[i], r, t)

    def r1_start(i, _):
        r1_copy(i).start()
        return 0

    lax.fori_loop(1, nc, r1_start, 0)
    red1[pl.ds(c, 1)] = chi[pl.ds(c, 1)]

    def r1_wait(i, _):
        r1_copy(i).wait_recv()
        return 0

    lax.fori_loop(1, nc, r1_wait, 0)
    part = red1[0]
    for k in range(1, nc):
        part = part + red1[k]
    wc = total_ri // nr
    for s in range(nr):
        st2[s] = part[:, s * wc:(s + 1) * wc]

    def r2_copy(i):
        t = lax.rem(r + i, nr)
        return remote(st2.at[t], red2.at[r], r2_send.at[i], r2_recv.at[i], t, c)

    for i in range(1, nr):
        r2_copy(i).start()
    red2[pl.ds(r, 1)] = st2[pl.ds(r, 1)]
    for i in range(1, nr):
        r2_copy(i).wait_recv()
    acc = red2[0]
    for k in range(1, nr):
        acc = acc + red2[k]
    out_ref[...] = acc

    for kind in (0, 1):
        def g_sent(i, _):
            g_copy(i, kind).wait_send()
            return 0
        lax.fori_loop(1, nc, g_sent, 0)

    def v_sent(i, _):
        v_copy(i).wait_send()
        return 0

    lax.fori_loop(1, n_dev, v_sent, 0)

    def col_sent(i, _):
        o_copy(i).wait_send()
        r1_copy(i).wait_send()
        return 0

    lax.fori_loop(1, nc, col_sent, 0)
    for i in range(1, nr):
        r2_copy(i).wait_send()


def body(nr, nc, b_tensor, ri_pairs, g_occ, g_vir, occ_mask, vir_mask):
    np_, rows, n = b_tensor.shape
    w = n // nc
    q = BS // w
    pc = rows // nc
    total_ri = nc * np_

    def pack(g):
        return jnp.concatenate([g[i * (n // q):(i + 1) * (n // q)] for i in range(q)], axis=1)

    vmem = pl.BlockSpec(memory_space=pltpu.VMEM)
    smem = pl.BlockSpec(memory_space=pltpu.SMEM)
    bf16, f32 = jnp.bfloat16, jnp.float32
    dma = pltpu.SemaphoreType.DMA
    return pl.pallas_call(
        functools.partial(kernel, nr, nc),
        out_shape=jax.ShapeDtypeStruct((np_, total_ri // nr), f32),
        in_specs=[smem, smem, smem, vmem, vmem, vmem],
        out_specs=vmem,
        scratch_shapes=[
            pltpu.VMEM((nc, n // q, BS), bf16),
            pltpu.VMEM((nc, n // q, BS), bf16),
            pltpu.VMEM((n, n), bf16),
            pltpu.VMEM((n, n), bf16),
            pltpu.VMEM((nr, rows, np_, BS), f32),
            pltpu.VMEM((nr, rows, np_, BS), bf16),
            pltpu.VMEM((nr, rows, np_, BS), bf16),
            pltpu.VMEM((nr, pc, nc, np_, BS), bf16),
            pltpu.VMEM((nr, pc, nc, np_, BS), bf16),
            pltpu.VMEM((nc, np_, total_ri), f32),
            pltpu.VMEM((nc, np_, total_ri), f32),
            pltpu.VMEM((nr, np_, total_ri // nr), f32),
            pltpu.VMEM((nr, np_, total_ri // nr), f32),
            dma((2, nc)), dma((2, nc)),
            dma((nr * nc,)), dma((nr, nc)),
            dma((nc,)), dma((nc,)),
            dma((nc,)), dma((nc,)),
            dma((nr,)), dma((nr,)),
        ],
        compiler_params=pltpu.CompilerParams(
            collective_id=0, has_side_effects=True, vmem_limit_bytes=56 * 1024 * 1024),
    )(ri_pairs.reshape(-1), occ_mask.reshape(-1), vir_mask.reshape(-1), b_tensor, pack(g_occ), pack(g_vir))


def solution(mesh):
    in_specs = (
        P("col", "row", None),
        P("col", None, None),
        P(None, "col"),
        P(None, "col"),
        P(),
        P(),
    )
    return jax.shard_map(
        functools.partial(body, mesh.shape["row"], mesh.shape["col"]),
        mesh=mesh, in_specs=in_specs, out_specs=P("col", "row"), check_vma=False)
```

time: 206 us -> 89.5 us (0.43)
  waiting for transfers between devices: 127 us -> 0 us
  Pallas kernels: 0 us -> 80.9 us
  blocking collectives: 21.1 us -> 0 us
  between operations: 13.5 us -> 0.03 us
  starting transfers between devices: 13 us -> 0 us
  local copies, waits for them, and re-layouts: 20 us -> 7.43 us
  matrix products: 9.97 us -> 0 us
    pallas_call x0 -> x1, Pallas kernels: none -> 80.9 us  [body(): pl.pallas_call(functools.partial(kernel, nr, nc), out_shape=jax.ShapeDtyp...]
    all_to_all x3 -> x0, waiting for transfers between devices: 76.2 us -> none  [the longest x1 30.2 us: body(): lax.all_to_all(vir_side, 'row', split_axis=2, concat_axis=1, tiled=True)]
    reduce_scatter x1 -> x0, waiting for transfers between devices: 30.6 us -> none  [body(): lax.psum_scatter(lax.dot_general(occ_flat, vir_flat, (((1,), (1,)), ((),...]
    all_gather x2 -> x0, blocking collectives: 21.1 us -> none  [the longest x1 11.6 us: body(): lax.all_gather(g_vir, 'col', axis=1, tiled=True)]
    unnamed x3 -> x0, waiting for transfers between devices: 19.9 us -> none
    all_to_all x3 -> x0, starting transfers between devices: 12.9 us -> none  [the longest x1 5 us: body(): lax.all_to_all(vir_side, 'row', split_axis=2, concat_axis=1, tiled=True)]
    dot_general x3 -> x0, matrix products: 9.97 us -> none  [the longest x1 4.19 us: body(): jnp.einsum('lm,pnm->pln', occ_green, masked, preferred_element_type=jnp.f...]
    convert_element_type x5 -> x0, local copies, waits for them, and re-layouts: 7.87 us -> none  [the longest x1 4.49 us: body(): occ_side = jnp.einsum('lm,pnm->pln', occ_green, masked, preferred_element...]
  transfers between devices with their start and end apart: 5 -> 0, of which waited for: 5 -> 0; matrix products, arithmetic and copies ran while one was open for 8% -> 0% of each run, Pallas kernels for 0% -> 0%
where the time goes in v1:
time: 89.5 us; the launch traced here: 89.1 us
  Pallas kernels  80.9 us (90%)
  local copies, waits for them, and re-layouts  7.43 us (8%)
    pallas_call x1, Pallas kernels, body(): pl.pallas_call(functools.partial(kernel, nr, nc), out_shape=jax.ShapeDtyp...  80.9 us
    unnamed x6, local copies, waits for them, and re-layouts  2.55 us

profile of v1, /device:TPU:0, one launch (start us, length us, event | category | flops | bytes accessed | tf_op | source)
XLA Modules:
  0.0 89.1 jit_solution(9321716256616385492)
XLA Ops:
  0.0 0.8 fusion.1
  0.8 0.1 copy.16
  0.9 0.1 copy.17
  1.0 0.8 fusion
  1.8 0.1 copy.18
  1.9 0.1 copy.19
  2.0 0.8 pad_maximum_fusion
  2.8 0.8 copy.11
  3.6 0.7 reshape.9.ri_ref
  4.3 1.3 %reshape.10.om_ref = s32[16]{0:T(128)} reshape(s32[4,4]{1,0:T(4,128)} %param.10) | data formatting | bytes 128 | tf_op jit(solution)/shard_map/reshape | solution.py:260
  5.6 1.3 %reshape.11.vm_ref = s32[16]{0:T(128)} reshape(s32[4,4]{1,0:T(4,128)} %param.11) | data formatting | bytes 128 | tf_op jit(solution)/shard_map/reshape | solution.py:260
  6.9 80.9 %shard_map.64 = f32[16,32]{1,0:T(8,128)} custom-call(s32[256]{0:T(256)} %reshape.9.ri_ref, s32[16]{0:T(128)} %reshape.10.om_ref, s32[16]{0:T(128)} %reshape.11.vm_ref, bf16[16,128,512]{2,1,0:T(8,128)(2,1)} %b_ref.1, bf16[256,128]{1,0:T(8,128)(2,1)} %get-tuple-element.9.go_ref, bf16[256,128]{1,0:T(8,128)(2,1)} %get-tuple-element.10.gv_ref), custom_call_target="tpu_custom_call" | custom-call | tf_op jit(solution)/shard_map/pallas_call | solution.py:233
  87.8 1.3 %copy.21 = f32[16,32]{1,0:T(8,128)} copy(f32[16,32]{1,0:T(8,128)} %shard_map.64) | data formatting | bytes 4096

commit v2 on v1

v2 whole, which is shorter than its diff:
```python
import functools

import jax
import jax.numpy as jnp
from jax import lax
from jax.experimental import pallas as pl
from jax.experimental.pallas import tpu as pltpu
from jax.sharding import PartitionSpec as P

BS = 128


def kernel(nr, nc, ri_ref, om_ref, vm_ref, b_hbm, go_ref, gv_ref, out_ref,
           b_ref, gv_slots, go_slots, gv, go, wide, v16, o16, vir_all, occ_all,
           chi, red1, st2, red2,
           b_sem, g_send, g_recv, v_send, v_recv, o_send, o_recv,
           r1_send, r1_recv, r2_send, r2_recv):
    r = lax.axis_index("row")
    c = lax.axis_index("col")
    me = r * nc + c
    n_dev = nr * nc
    np_, rows, n = b_ref.shape
    na = n // BS
    pc = rows // nc
    w = n // nc

    def remote(src, dst, send, recv, row, col):
        return pltpu.make_async_remote_copy(
            src_ref=src, dst_ref=dst, send_sem=send, recv_sem=recv,
            device_id={"row": row, "col": col}, device_id_type=pl.DeviceIdType.MESH)

    fetch = pltpu.make_async_copy(b_hbm, b_ref, b_sem)
    fetch.start()
    barrier = pltpu.get_barrier_semaphore()

    def greet(i, _):
        t = lax.rem(me + i, n_dev)
        pl.semaphore_signal(barrier, inc=1,
                            device_id={"row": t // nc, "col": lax.rem(t, nc)},
                            device_id_type=pl.DeviceIdType.MESH)
        return 0

    lax.fori_loop(1, n_dev, greet, 0)
    for src, slots in ((gv_ref, gv_slots), (go_ref, go_slots)):
        slots[pl.ds(c, 1)] = src[...][None]
    pl.semaphore_wait(barrier, n_dev - 1)

    def g_copy(i, kind):
        t = lax.rem(c + i, nc)
        slots = gv_slots if kind == 0 else go_slots
        return remote(slots.at[c], slots.at[c], g_send.at[kind, i], g_recv.at[kind, i], r, t)

    def g_begin(kind):
        def g_start(i, _):
            g_copy(i, kind).start()
            return 0
        lax.fori_loop(1, nc, g_start, 0)

    def assemble(kind, slots, mask, store):
        def g_wait(i, _):
            g_copy(i, kind).wait_recv()
            return 0
        lax.fori_loop(1, nc, g_wait, 0)
        per = BS // w
        for j in range(na):
            block = slots[j * per:(j + 1) * per].reshape(BS, n)
            for i in range(na):
                m = mask[i, j].astype(jnp.float32)
                piece = block[:, i * BS:(i + 1) * BS].astype(jnp.float32) * m
                store(i * BS, j, piece.astype(jnp.bfloat16).T)

    def gv_store(first, j, piece):
        gv[j // 2, first:first + BS, (j % 2) * BS:(j % 2 + 1) * BS] = piece

    def go_store(first, j, piece):
        go[first:first + BS, j * BS:(j + 1) * BS] = piece

    g_begin(0)
    fetch.wait()
    for p in range(np_):
        row = jnp.concatenate(
            [jnp.full((1, BS), ri_ref[r, j, p].astype(jnp.float32)) for j in range(na)], axis=1)
        b_ref[p] = (b_ref[p].astype(jnp.float32) * row).astype(jnp.bfloat16)
    assemble(0, gv_slots, vm_ref, gv_store)
    g_begin(1)

    def round_rows(dst, s):
        def one(i, _):
            dst[s, pl.ds(i * pc, pc)] = wide[s, pl.ds(i * pc, pc)].astype(jnp.bfloat16)
            return 0
        lax.fori_loop(0, nc, one, 0)

    halves = na // 2
    group = 4

    def v_copy(s, tc):
        return remote(v16.at[s, pl.ds(tc * pc, pc)], vir_all.at[r, :, c],
                      v_send.at[s, tc], v_recv.at[r, c], s, tc)

    for t in range(halves):
        half = lax.rem(r // 2 + 1 + t, halves)
        for g in range(np_ // group):
            lhs = b_ref[g * group:(g + 1) * group].reshape(group * rows, n)
            res = jnp.dot(lhs, gv[half], preferred_element_type=jnp.float32)
            for k in range(group):
                for e in range(2):
                    wide[2 * half + e, :, g * group + k, :] = res[
                        k * rows:(k + 1) * rows, e * BS:(e + 1) * BS]
        for e in range(2):
            s = 2 * half + e
            round_rows(v16, s)
            first = (s == r).astype(jnp.int32)

            def v_start(i, _):
                v_copy(s, lax.rem(c + i, nc)).start()
                return 0

            lax.fori_loop(first, nc, v_start, 0)
    vir_all[pl.ds(r, 1), :, pl.ds(c, 1)] = v16[pl.ds(r, 1), pl.ds(c * pc, pc)][:, :, None]

    assemble(1, go_slots, om_ref, go_store)
    for g in range(np_ // 2):
        rhs = b_ref[2 * g:2 * g + 2].reshape(2 * rows, n)
        res = lax.dot_general(go[...], rhs, (((1,), (1,)), ((), ())),
                              preferred_element_type=jnp.float32)
        for k in range(2):
            for s in range(nr):
                wide[s, :, 2 * g + k, :] = res[s * BS:(s + 1) * BS, k * BS:(k + 1) * BS]
    for s in range(nr):
        round_rows(o16, s)

    def o_copy(i):
        t = lax.rem(c + i, nc)
        return remote(o16.at[:, pl.ds(t * pc, pc)], occ_all.at[:, :, c],
                      o_send.at[i], o_recv.at[i], r, t)

    def o_start(i, _):
        o_copy(i).start()
        return 0

    lax.fori_loop(1, nc, o_start, 0)
    occ_all[:, :, pl.ds(c, 1)] = o16[:, pl.ds(c * pc, pc)][:, :, None]

    def o_wait(i, _):
        o_copy(i).wait_recv()
        return 0

    lax.fori_loop(1, nc, o_wait, 0)

    total_ri = nc * np_
    chi[...] = jnp.zeros_like(chi)
    step = min(pc, 8)
    for off in range(nr):
        rr = lax.rem(r + off, nr)

        def v_wait(j, _):
            col = lax.rem(c + j, nc)
            remote(v16.at[0, pl.ds(0, pc)], vir_all.at[rr, :, col],
                   v_send.at[0, 0], v_recv.at[rr, col], rr, col).wait_recv()
            return 0

        lax.fori_loop(1 if off == 0 else 0, nc, v_wait, 0)
        for k in range(0, pc, step):
            left = occ_all[rr, k:k + step].reshape(step, total_ri, BS)
            right = vir_all[rr, k:k + step].reshape(step, total_ri, BS)
            left = jnp.concatenate([left[i] for i in range(step)], axis=1)
            right = jnp.concatenate([right[i] for i in range(step)], axis=1)
            chi[...] += lax.dot_general(
                left, right, (((1,), (1,)), ((), ())),
                preferred_element_type=jnp.float32).reshape(nc, np_, total_ri)

    def r1_copy(i):
        t = lax.rem(c + i, nc)
        return remote(chi.at[t], red1.at[c], r1_send.at[i], r1_recv.at[i], r, t)

    def r1_start(i, _):
        r1_copy(i).start()
        return 0

    lax.fori_loop(1, nc, r1_start, 0)
    red1[pl.ds(c, 1)] = chi[pl.ds(c, 1)]

    def r1_wait(i, _):
        r1_copy(i).wait_recv()
        return 0

    lax.fori_loop(1, nc, r1_wait, 0)
    part = red1[0]
    for k in range(1, nc):
        part = part + red1[k]
    wc = total_ri // nr
    for s in range(nr):
        st2[s] = part[:, s * wc:(s + 1) * wc]

    def r2_copy(i):
        t = lax.rem(r + i, nr)
        return remote(st2.at[t], red2.at[r], r2_send.at[i], r2_recv.at[i], t, c)

    for i in range(1, nr):
        r2_copy(i).start()
    red2[pl.ds(r, 1)] = st2[pl.ds(r, 1)]
    for i in range(1, nr):
        r2_copy(i).wait_recv()
    acc = red2[0]
    for k in range(1, nr):
        acc = acc + red2[k]
    out_ref[...] = acc

    for kind in (0, 1):
        def g_sent(i, _):
            g_copy(i, kind).wait_send()
            return 0
        lax.fori_loop(1, nc, g_sent, 0)

    def v_sent(i, _):
        t = lax.rem(me + i, n_dev)
        v_copy(t // nc, lax.rem(t, nc)).wait_send()
        return 0

    lax.fori_loop(1, n_dev, v_sent, 0)

    def col_sent(i, _):
        o_copy(i).wait_send()
        r1_copy(i).wait_send()
        return 0

    lax.fori_loop(1, nc, col_sent, 0)
    for i in range(1, nr):
        r2_copy(i).wait_send()


def body(nr, nc, b_tensor, ri_pairs, g_occ, g_vir, occ_mask, vir_mask):
    np_, rows, n = b_tensor.shape
    w = n // nc
    pc = rows // nc
    total_ri = nc * np_

    vmem = pl.BlockSpec(memory_space=pltpu.VMEM)
    smem = pl.BlockSpec(memory_space=pltpu.SMEM)
    bf16, f32 = jnp.bfloat16, jnp.float32
    dma = pltpu.SemaphoreType.DMA
    return pl.pallas_call(
        functools.partial(kernel, nr, nc),
        out_shape=jax.ShapeDtypeStruct((np_, total_ri // nr), f32),
        in_specs=[smem, smem, smem, pl.BlockSpec(memory_space=pl.ANY), vmem, vmem],
        out_specs=vmem,
        scratch_shapes=[
            pltpu.VMEM((np_, rows, n), bf16),
            pltpu.VMEM((nc, w, n), bf16),
            pltpu.VMEM((nc, w, n), bf16),
            pltpu.VMEM((n // (2 * BS), n, 2 * BS), bf16),
            pltpu.VMEM((n, n), bf16),
            pltpu.VMEM((nr, rows, np_, BS), f32),
            pltpu.VMEM((nr, rows, np_, BS), bf16),
            pltpu.VMEM((nr, rows, np_, BS), bf16),
            pltpu.VMEM((nr, pc, nc, np_, BS), bf16),
            pltpu.VMEM((nr, pc, nc, np_, BS), bf16),
            pltpu.VMEM((nc, np_, total_ri), f32),
            pltpu.VMEM((nc, np_, total_ri), f32),
            pltpu.VMEM((nr, np_, total_ri // nr), f32),
            pltpu.VMEM((nr, np_, total_ri // nr), f32),
            dma, dma((2, nc)), dma((2, nc)),
            dma((nr, nc)), dma((nr, nc)),
            dma((nc,)), dma((nc,)),
            dma((nc,)), dma((nc,)),
            dma((nr,)), dma((nr,)),
        ],
        compiler_params=pltpu.CompilerParams(
            collective_id=0, has_side_effects=True, vmem_limit_bytes=56 * 1024 * 1024),
    )(ri_pairs.transpose(1, 2, 0), occ_mask, vir_mask, b_tensor, g_occ.T, g_vir.T)


def solution(mesh):
    in_specs = (
        P("col", "row", None),
        P("col", None, None),
        P(None, "col"),
        P(None, "col"),
        P(),
        P(),
    )
    return jax.shard_map(
        functools.partial(body, mesh.shape["row"], mesh.shape["col"]),
        mesh=mesh, in_specs=in_specs, out_specs=P("col", "row"), check_vma=False)
```

time: 89.5 us -> 81.5 us (0.911)
  local copies, waits for them, and re-layouts: 7.43 us -> 1.3 us
  Pallas kernels: 80.9 us -> 80 us
    reshape x3 -> x0, local copies, waits for them, and re-layouts: 3.31 us -> none  [the longest x1 1.34 us: body(): occ_mask.reshape(-1)]
    slice x2 -> x0, local copies, waits for them, and re-layouts: 1.56 us -> none  [pack(): g[i * (n // q):(i + 1) * (n // q)]]
    unnamed x6 -> x1, local copies, waits for them, and re-layouts: 2.55 us -> 1.3 us
    pallas_call x1, Pallas kernels: 80.9 us -> 80 us  [body(): pl.pallas_call(functools.partial(kernel, nr, nc), out_shape=jax.ShapeDtyp...]
where the time goes in v2:
time: 81.5 us; the launch traced here: 81.3 us
  Pallas kernels  80 us (98%)
  local copies, waits for them, and re-layouts  1.3 us (2%)
    pallas_call x1, Pallas kernels, body(): pl.pallas_call(functools.partial(kernel, nr, nc), out_shape=jax.ShapeDtyp...  80 us

profile of v2, /device:TPU:0, one launch (start us, length us, event | category | flops | bytes accessed | tf_op | source)
XLA Modules:
  0.0 81.3 jit_solution(8095694723913119935)
XLA Ops:
  0.0 80.0 %shard_map.64 = f32[16,32]{1,0:T(8,128)} custom-call(s32[4,4,16]{2,1,0:T(4,128)} %bitcast.5, s32[4,4]{1,0:T(4,128)} %om_ref.1, s32[4,4]{1,0:T(4,128)} %vm_ref.1, bf16[16,128,512]{2,1,0:T(8,128)(2,1)} %b_hbm.1, bf16[64,512]{1,0:T(8,128)(2,1)} %bitcast.3, bf16[64,512]{1,0:T(8,128)(2,1)} %bitcast.4), custom_call_target="tpu_custom_call" | custom-call | tf_op jit(solution)/shard_map/pallas_call | solution.py:242
  80.0 1.3 %copy.8 = f32[16,32]{1,0:T(8,128)} copy(f32[16,32]{1,0:T(8,128)} %shard_map.64) | data formatting | bytes 4096

commit v3 on v2

--- a/solution.py
+++ b/solution.py
@@ -56,33 +56,42 @@
             return 0
         lax.fori_loop(1, nc, g_start, 0)
 
-    def assemble(kind, slots, mask, store):
+    per = BS // w
+    shards = 2 * per
+
+    def arrived(kind, half=None):
         def g_wait(i, _):
-            g_copy(i, kind).wait_recv()
+            if half is None:
+                g_copy(i, kind).wait_recv()
+            else:
+                @pl.when(lax.rem(c + nc - i, nc) // shards == half)
+                def _():
+                    g_copy(i, kind).wait_recv()
             return 0
         lax.fori_loop(1, nc, g_wait, 0)
-        per = BS // w
-        for j in range(na):
-            block = slots[j * per:(j + 1) * per].reshape(BS, n)
-            for i in range(na):
-                m = mask[i, j].astype(jnp.float32)
-                piece = block[:, i * BS:(i + 1) * BS].astype(jnp.float32) * m
-                store(i * BS, j, piece.astype(jnp.bfloat16).T)
-
-    def gv_store(first, j, piece):
-        gv[j // 2, first:first + BS, (j % 2) * BS:(j % 2 + 1) * BS] = piece
+
+    def assemble(slots, mask, j, store):
+        block = slots[pl.ds(j * per, per)].reshape(BS, n)
+        for i in range(na):
+            m = mask[i, j].astype(jnp.float32)
+            piece = block[:, i * BS:(i + 1) * BS].astype(jnp.float32) * m
+            store(i * BS, j, piece.astype(jnp.bfloat16).T)
 
     def go_store(first, j, piece):
         go[first:first + BS, j * BS:(j + 1) * BS] = piece
 
-    g_begin(0)
+    halves = na // 2
+    far = lax.rem(r // 2 + 1, halves)
+
+    @pl.when(c // shards == far)
+    def _():
+        g_begin(0)
+
     fetch.wait()
     for p in range(np_):
         row = jnp.concatenate(
             [jnp.full((1, BS), ri_ref[r, j, p].astype(jnp.float32)) for j in range(na)], axis=1)
         b_ref[p] = (b_ref[p].astype(jnp.float32) * row).astype(jnp.bfloat16)
-    assemble(0, gv_slots, vm_ref, gv_store)
-    g_begin(1)
 
     def round_rows(dst, s):
         def one(i, _):
@@ -90,15 +99,26 @@
             return 0
         lax.fori_loop(0, nc, one, 0)
 
-    halves = na // 2
     group = 4
 
     def v_copy(s, tc):
-        return remote(v16.at[s, pl.ds(tc * pc, pc)], vir_all.at[r, :, c],
+        return remote(v16.at[s, pl.ds(tc * pc, pc)], vir_all.at[r, c],
                       v_send.at[s, tc], v_recv.at[r, c], s, tc)
 
     for t in range(halves):
-        half = lax.rem(r // 2 + 1 + t, halves)
+        half = lax.rem(far + t, halves)
+        arrived(0, half)
+        for e in range(2):
+            def gv_store(first, j, piece, e=e):
+                gv[half, first:first + BS, e * BS:(e + 1) * BS] = piece
+
+            assemble(gv_slots, vm_ref, 2 * half + e, gv_store)
+        if t == 0:
+            @pl.when(c // shards != far)
+            def _():
+                g_begin(0)
+
+            g_begin(1)
         for g in range(np_ // group):
             lhs = b_ref[g * group:(g + 1) * group].reshape(group * rows, n)
             res = jnp.dot(lhs, gv[half], preferred_element_type=jnp.float32)
@@ -107,7 +127,7 @@
                     wide[2 * half + e, :, g * group + k, :] = res[
                         k * rows:(k + 1) * rows, e * BS:(e + 1) * BS]
         for e in range(2):
-            s = 2 * half + e
+            s = 2 * half + jnp.where(half > r // 2, 1 - e, e)
             round_rows(v16, s)
             first = (s == r).astype(jnp.int32)
 
@@ -116,9 +136,11 @@
                 return 0
 
             lax.fori_loop(first, nc, v_start, 0)
-    vir_all[pl.ds(r, 1), :, pl.ds(c, 1)] = v16[pl.ds(r, 1), pl.ds(c * pc, pc)][:, :, None]
-
-    assemble(1, go_slots, om_ref, go_store)
+    vir_all[pl.ds(r, 1), pl.ds(c, 1)] = v16[pl.ds(r, 1), pl.ds(c * pc, pc)][:, None]
+
+    arrived(1)
+    for j in range(na):
+        assemble(go_slots, om_ref, j, go_store)
     for g in range(np_ // 2):
         rhs = b_ref[2 * g:2 * g + 2].reshape(2 * rows, n)
         res = lax.dot_general(go[...], rhs, (((1,), (1,)), ((), ())),
@@ -131,7 +153,7 @@
 
     def o_copy(i):
         t = lax.rem(c + i, nc)
-        return remote(o16.at[:, pl.ds(t * pc, pc)], occ_all.at[:, :, c],
+        return remote(o16.at[:, pl.ds(t * pc, pc)], occ_all.at[:, c],
                       o_send.at[i], o_recv.at[i], r, t)
 
     def o_start(i, _):
@@ -139,7 +161,7 @@
         return 0
 
     lax.fori_loop(1, nc, o_start, 0)
-    occ_all[:, :, pl.ds(c, 1)] = o16[:, pl.ds(c * pc, pc)][:, :, None]
+    occ_all[:, pl.ds(c, 1)] = o16[:, pl.ds(c * pc, pc)][:, None]
 
     def o_wait(i, _):
         o_copy(i).wait_recv()
@@ -155,16 +177,15 @@
 
         def v_wait(j, _):
             col = lax.rem(c + j, nc)
-            remote(v16.at[0, pl.ds(0, pc)], vir_all.at[rr, :, col],
+            remote(v16.at[0, pl.ds(0, pc)], vir_all.at[rr, col],
                    v_send.at[0, 0], v_recv.at[rr, col], rr, col).wait_recv()
             return 0
 
         lax.fori_loop(1 if off == 0 else 0, nc, v_wait, 0)
         for k in range(0, pc, step):
-            left = occ_all[rr, k:k + step].reshape(step, total_ri, BS)
-            right = vir_all[rr, k:k + step].reshape(step, total_ri, BS)
-            left = jnp.concatenate([left[i] for i in range(step)], axis=1)
-            right = jnp.concatenate([right[i] for i in range(step)], axis=1)
+            left, right = (
+                jnp.concatenate([full[rr, :, k + i].reshape(total_ri, BS) for i in range(step)], axis=1)
+                for full in (occ_all, vir_all))
             chi[...] += lax.dot_general(
                 left, right, (((1,), (1,)), ((), ())),
                 preferred_element_type=jnp.float32).reshape(nc, np_, total_ri)
@@ -253,8 +274,8 @@
             pltpu.VMEM((nr, rows, np_, BS), f32),
             pltpu.VMEM((nr, rows, np_, BS), bf16),
             pltpu.VMEM((nr, rows, np_, BS), bf16),
-            pltpu.VMEM((nr, pc, nc, np_, BS), bf16),
-            pltpu.VMEM((nr, pc, nc, np_, BS), bf16),
+            pltpu.VMEM((nr, nc, pc, np_, BS), bf16),
+            pltpu.VMEM((nr, nc, pc, np_, BS), bf16),
             pltpu.VMEM((nc, np_, total_ri), f32),
             pltpu.VMEM((nc, np_, total_ri), f32),
             pltpu.VMEM((nr, np_, total_ri // nr), f32),

time: 81.5 us -> 84.8 us (1.040)
  Pallas kernels: 80 us -> 83.3 us
    pallas_call x1, Pallas kernels: 80 us -> 83.3 us  [body(): pl.pallas_call(functools.partial(kernel, nr, nc), out_shape=jax.ShapeDtyp...]
where the time goes in v3:
time: 84.8 us; the launch traced here: 84.6 us
  Pallas kernels  83.3 us (98%)
  local copies, waits for them, and re-layouts  1.3 us (2%)
    pallas_call x1, Pallas kernels, body(): pl.pallas_call(functools.partial(kernel, nr, nc), out_shape=jax.ShapeDtyp...  83.3 us

profile of v3, /device:TPU:0, one launch (start us, length us, event | category | flops | bytes accessed | tf_op | source)
XLA Modules:
  0.0 84.6 jit_solution(18332795168491592107)
XLA Ops:
  0.0 83.3 %shard_map.64 = f32[16,32]{1,0:T(8,128)} custom-call(s32[4,4,16]{2,1,0:T(4,128)} %bitcast.5, s32[4,4]{1,0:T(4,128)} %om_ref.1, s32[4,4]{1,0:T(4,128)} %vm_ref.1, bf16[16,128,512]{2,1,0:T(8,128)(2,1)} %b_hbm.1, bf16[64,512]{1,0:T(8,128)(2,1)} %bitcast.3, bf16[64,512]{1,0:T(8,128)(2,1)} %bitcast.4), custom_call_target="tpu_custom_call" | custom-call | tf_op jit(solution)/shard_map/pallas_call | solution.py:263
  83.3 1.3 %copy.8 = f32[16,32]{1,0:T(8,128)} copy(f32[16,32]{1,0:T(8,128)} %shard_map.64) | data formatting | bytes 4096

commit v4 on v2

--- a/solution.py
+++ b/solution.py
@@ -94,7 +94,7 @@
     group = 4
 
     def v_copy(s, tc):
-        return remote(v16.at[s, pl.ds(tc * pc, pc)], vir_all.at[r, :, c],
+        return remote(v16.at[s, pl.ds(tc * pc, pc)], vir_all.at[r, c],
                       v_send.at[s, tc], v_recv.at[r, c], s, tc)
 
     for t in range(halves):
@@ -116,7 +116,7 @@
                 return 0
 
             lax.fori_loop(first, nc, v_start, 0)
-    vir_all[pl.ds(r, 1), :, pl.ds(c, 1)] = v16[pl.ds(r, 1), pl.ds(c * pc, pc)][:, :, None]
+    vir_all[pl.ds(r, 1), pl.ds(c, 1)] = v16[pl.ds(r, 1), pl.ds(c * pc, pc)][:, None]
 
     assemble(1, go_slots, om_ref, go_store)
     for g in range(np_ // 2):
@@ -131,7 +131,7 @@
 
     def o_copy(i):
         t = lax.rem(c + i, nc)
-        return remote(o16.at[:, pl.ds(t * pc, pc)], occ_all.at[:, :, c],
+        return remote(o16.at[:, pl.ds(t * pc, pc)], occ_all.at[:, c],
                       o_send.at[i], o_recv.at[i], r, t)
 
     def o_start(i, _):
@@ -139,7 +139,7 @@
         return 0
 
     lax.fori_loop(1, nc, o_start, 0)
-    occ_all[:, :, pl.ds(c, 1)] = o16[:, pl.ds(c * pc, pc)][:, :, None]
+    occ_all[:, pl.ds(c, 1)] = o16[:, pl.ds(c * pc, pc)][:, None]
 
     def o_wait(i, _):
         o_copy(i).wait_recv()
@@ -155,16 +155,15 @@
 
         def v_wait(j, _):
             col = lax.rem(c + j, nc)
-            remote(v16.at[0, pl.ds(0, pc)], vir_all.at[rr, :, col],
+            remote(v16.at[0, pl.ds(0, pc)], vir_all.at[rr, col],
                    v_send.at[0, 0], v_recv.at[rr, col], rr, col).wait_recv()
             return 0
 
         lax.fori_loop(1 if off == 0 else 0, nc, v_wait, 0)
         for k in range(0, pc, step):
-            left = occ_all[rr, k:k + step].reshape(step, total_ri, BS)
-            right = vir_all[rr, k:k + step].reshape(step, total_ri, BS)
-            left = jnp.concatenate([left[i] for i in range(step)], axis=1)
-            right = jnp.concatenate([right[i] for i in range(step)], axis=1)
+            left, right = (
+                jnp.concatenate([full[rr, :, k + i].reshape(total_ri, BS) for i in range(step)], axis=1)
+                for full in (occ_all, vir_all))
             chi[...] += lax.dot_general(
                 left, right, (((1,), (1,)), ((), ())),
                 preferred_element_type=jnp.float32).reshape(nc, np_, total_ri)
@@ -253,8 +252,8 @@
             pltpu.VMEM((nr, rows, np_, BS), f32),
             pltpu.VMEM((nr, rows, np_, BS), bf16),
             pltpu.VMEM((nr, rows, np_, BS), bf16),
-            pltpu.VMEM((nr, pc, nc, np_, BS), bf16),
-            pltpu.VMEM((nr, pc, nc, np_, BS), bf16),
+            pltpu.VMEM((nr, nc, pc, np_, BS), bf16),
+            pltpu.VMEM((nr, nc, pc, np_, BS), bf16),
             pltpu.VMEM((nc, np_, total_ri), f32),
             pltpu.VMEM((nc, np_, total_ri), f32),
             pltpu.VMEM((nr, np_, total_ri // nr), f32),

time: 81.5 us -> 81.5 us (level)
  no operation moved by 1% of the time
where the time goes in v4:
time: 81.5 us; the launch traced here: 81.3 us
  Pallas kernels  80 us (98%)
  local copies, waits for them, and re-layouts  1.3 us (2%)
    pallas_call x1, Pallas kernels, body(): pl.pallas_call(functools.partial(kernel, nr, nc), out_shape=jax.ShapeDtyp...  80 us

profile of v4, /device:TPU:0, one launch (start us, length us, event | category | flops | bytes accessed | tf_op | source)
XLA Modules:
  0.0 81.3 jit_solution(13486316230363033173)
XLA Ops:
  0.0 80.0 %shard_map.64 = f32[16,32]{1,0:T(8,128)} custom-call(s32[4,4,16]{2,1,0:T(4,128)} %bitcast.5, s32[4,4]{1,0:T(4,128)} %om_ref.1, s32[4,4]{1,0:T(4,128)} %vm_ref.1, bf16[16,128,512]{2,1,0:T(8,128)(2,1)} %b_hbm.1, bf16[64,512]{1,0:T(8,128)(2,1)} %bitcast.3, bf16[64,512]{1,0:T(8,128)(2,1)} %bitcast.4), custom_call_target="tpu_custom_call" | custom-call | tf_op jit(solution)/shard_map/pallas_call | solution.py:241
  80.0 1.3 %copy.8 = f32[16,32]{1,0:T(8,128)} copy(f32[16,32]{1,0:T(8,128)} %shard_map.64) | data formatting | bytes 4096
